TPU v7x, 128 devices: a whole 4x4x4 slice. The times are simulated.
128 devices in a mesh: dp: 8 (over z, core), ctx: 16 (over x, y).
Axes of the slice: x: 4, y: 4, z: 4, core: 2. Of those that a mesh axis runs over, the one named last changes fastest.
Arguments:
- queries: bfloat16 [32768, 1024], P(('dp', 'ctx')), may hold values from -27 to 27, as said below
- keys: bfloat16 [32768, 128], P(('dp', 'ctx')), may hold values from -4 to 4, as said below
- values: bfloat16 [32768, 128], P(('dp', 'ctx')), may hold values from -6 to 6
- grad_out: bfloat16 [32768, 1024], P(('dp', 'ctx')), may hold values from -6 to 6
- lengths: int32 [32], replicated, may hold values from 1 to 4096, 32768 in all
Outputs:
- attn_out: bfloat16 [32768, 1024], P(('dp', 'ctx'))
- grad_queries: bfloat16 [32768, 1024], P(('dp', 'ctx'))
- grad_keys: bfloat16 [32768, 128], P(('dp', 'ctx'))
- grad_values: bfloat16 [32768, 128], P(('dp', 'ctx'))
Inputs may be any that keep to these rules, and one draw needn't show every extreme that they name: `queries`: query entries lie in this range. `keys`: key entries lie in this range.
All inputs are finite; a program needn't handle non-finite values.
Results may differ from a plain program's by a relative error of at most 0.029.
Values may be sent and summed in bfloat16 or wider, within the bound.
A program may use at most 192 MiB of HBM per device.

v0:
```python
import functools
import math

import jax
import jax.numpy as jnp
from jax import lax
from jax.experimental import pallas as pl
from jax.experimental.pallas import tpu as pltpu
from jax.sharding import PartitionSpec as P

HEADS = 8
HDIM = 128
ROWS = 256
NDOCS = 32
SCALE = float(HDIM) ** -0.5
LOG2_SCALE = SCALE * math.log2(math.e)
BIG = 2.0**20
MESH = pl.DeviceIdType.MESH
F32 = jnp.float32
BF16 = jnp.bfloat16
FWD_UNROLL = 2
COMM = True


def dot(a, b, ca, cb):
    return lax.dot_general(a, b, (((ca,), (cb,)), ((), ())), preferred_element_type=F32)


def kernel(
    len_ref, q_ref, k_ref, v_ref, g_ref, o_ref, dq_ref, dk_ref, dv_ref,
    kb, vb, fk, qa, qt, gh, gs, gt, eb, db, mb, acc, lse, corr,
    pk, pv, rk, rv, rk2, rv2, rk3, rv3, ak, av, sk, sv, sk3, sv3,
    loc, kc, vc, kx, ky, vy, vx, bky, bvx, bkx, bvy, bkc, bvc,
):
    dp, ctx = lax.axis_index("dp"), lax.axis_index("ctx")
    x, y = ctx // 4, lax.rem(ctx, 4)
    block = dp * 16 + ctx
    ahead = (lax.rem(dp + 1, 8), ctx)
    behind = (lax.rem(dp + 7, 8), ctx)

    def along_x(i):
        return (dp, lax.rem(x + i + 4, 4) * 4 + y)

    def along_y(j):
        return (dp, x * 4 + lax.rem(y + j + 4, 4))

    def remote(src, dst, sems, index, device):
        return pltpu.make_async_remote_copy(
            src_ref=src, dst_ref=dst, send_sem=sems.at[(0,) + index], recv_sem=sems.at[(1,) + index],
            device_id=device, device_id_type=MESH,
        )

    own = [
        pltpu.make_async_copy(k_ref, kb.at[4], loc.at[0]),
        pltpu.make_async_copy(v_ref, vb.at[y * 5 + 4], loc.at[1]),
    ]
    for copy in own:
        copy.start()
    if COMM:
        barrier = pltpu.get_barrier_semaphore()
        for device in [along_x(1), along_x(2), along_x(3), along_y(1), along_y(2), along_y(3), ahead, behind]:
            pl.semaphore_signal(barrier, inc=1, device_id=device, device_id_type=MESH)
    for copy in own:
        copy.wait()

    def k_cross():
        return remote(k_ref, kb.at[0], kc, (0,), ahead)

    def v_cross():
        return remote(v_ref, vb.at[y * 5], vc, (0,), ahead)

    def k_x(i):
        wrap = (x + i >= 4).astype(jnp.int32)
        return remote(kb.at[4 - 4 * wrap], kb.at[4 - i], kx, (i - 1,), along_x(i))

    def k_y(j, r):
        wrap = (y + j >= 4).astype(jnp.int32)
        return remote(kb.at[r - wrap], kb.at[4 * j + r], ky, (j - 1, r - 1), along_y(j))

    def v_y(j, old):
        slot = y * 5 + (0 if old else 4)
        return remote(vb.at[slot], vb.at[slot], vy, (j - 1, old), along_y(j))

    def v_x(i, c):
        wrap = (x + i >= 4).astype(jnp.int32)
        return remote(vb.at[c * 5 + 4 - 4 * wrap], vb.at[c * 5 + 4 - i], vx, (i - 1, c), along_x(i))

    if COMM:
        pl.semaphore_wait(barrier, 8)
        k_cross().start()
        v_cross().start()
        for i in (1, 3, 2):
            @pl.when(x + i < 4)
            def _():
                k_x(i).start()
                v_x(i, y).start()
        for j in (1, 3, 2):
            v_y(j, 0).start()
            @pl.when(y + j < 4)
            def _():
                k_y(j, 4).start()

    lane = lax.broadcasted_iota(jnp.int32, (1, HDIM), 1)
    starts = jnp.zeros((1, HDIM), jnp.int32)
    stops = jnp.zeros((1, HDIM), jnp.int32)
    total = jnp.int32(0)
    for d in range(NDOCS):
        starts = jnp.where(lane == d, total, starts)
        total = total + len_ref[d]
        stops = jnp.where(lane == d, total, stops)
    place = lax.broadcasted_iota(jnp.int32, (ROWS, HDIM), 0)

    def member(start):
        position = place + start
        return (position >= starts) & (position < stops)

    query_member = jnp.where(member(block * ROWS), 1.0, 0.0).astype(BF16)
    for h in range(HEADS):
        heads = pl.ds(h * HDIM, HDIM)
        query = q_ref[:, heads]
        qa[h, :, :HDIM] = query
        qa[h, :, HDIM:] = query_member
        qt[:, pl.ds(h * ROWS, ROWS)] = query.T
        gh[h] = g_ref[:, heads]

    @pl.loop(0, 17)
    def _(index):
        group = jnp.maximum(index - 1, 0) // 4
        back = group + 4 * (4 - (index - 4 * group))
        fk[index] = jnp.where(member((block - back) * ROWS), 0.0, -BIG).astype(BF16)

    ones = jnp.ones((ROWS, HDIM), BF16)

    def head_rows(h):
        return pl.ds(pl.multiple_of(h * ROWS, ROWS), ROWS)

    def forward(slot, k0, v0, blocks):
        def body(h, carry):
            scores = [
                dot(qa[h], jnp.concatenate([kb[k0 + n], fk[k0 + n]], axis=1), 1, 1) for n in range(blocks)
            ]
            if slot is None:
                row = lax.broadcasted_iota(jnp.int32, (ROWS, ROWS), 0)
                column = lax.broadcasted_iota(jnp.int32, (ROWS, ROWS), 1)
                scores = [jnp.where(column <= row, scores[0], -BIG)]
            top = functools.reduce(jnp.maximum, [s[:, half] for s in scores for half in (slice(0, 128), slice(128, 256))])
            top = jnp.max(top, axis=1, keepdims=True)
            here = 0 if slot is None else slot
            if slot is None:
                peak = jnp.broadcast_to(top, (ROWS, HDIM))
            else:
                before = mb[here - 1, h]
                peak = jnp.maximum(before, top)
            mb[here, h] = peak
            peak2 = jnp.concatenate([peak, peak], axis=1) * LOG2_SCALE
            term = None
            for n in range(blocks):
                weights = jnp.exp2(scores[n] * LOG2_SCALE - peak2).astype(BF16)
                eb[k0 + n, head_rows(h), :] = weights
                part = dot(weights, jnp.concatenate([vb[v0 + n], ones], axis=1), 1, 0)
                term = part if term is None else term + part
            if slot is None:
                acc[h] = term
            else:
                shrink = jnp.exp2((before - peak) * LOG2_SCALE)
                acc[h] = acc[h] * jnp.concatenate([shrink, shrink], axis=1) + term
            return carry

        lax.fori_loop(0, HEADS, body, 0, unroll=FWD_UNROLL)

    forward(None, 4, y * 5 + 4, 1)

    if COMM:
        k_cross().wait_recv()
        v_cross().wait_recv()
        for i in (1, 3, 2):
            @pl.when(x + i >= 4)
            def _():
                k_x(i).start()
                v_x(i, y).start()
        for j in (1, 3, 2):
            v_y(j, 1).start()
        for i in (3, 1, 2):
            k_x(i).wait_recv()
        for r in (4, 3, 2, 1):
            for j in (1, 3, 2):
                if r == 4:
                    @pl.when(y + j >= 4)
                    def _():
                        k_y(j, 4).start()
                else:
                    k_y(j, r).start()
        for j in (1, 3, 2):
            for old in (0, 1):
                v_y(j, old).wait_recv()
        for j in (1, 3, 2):
            column = lax.rem(y - j + 4, 4)
            for i in (1, 3, 2):
                v_x(i, column).start()

    @pl.loop(0, 4)
    def _(j):
        column = lax.rem(y - j + 4, 4)
        wrap = (j > y).astype(jnp.int32)
        first = jnp.minimum(j, 1)
        if COMM:
            for i in (1, 2, 3):
                v_x(i, column).wait_recv()

            @pl.when(j > 0)
            def _():
                for r in (1, 2, 3, 4):
                    k_y(j, r).wait_recv()
        forward(j + 1, 4 * j + first, column * 5 + first - wrap, 4)

    for h in range(HEADS):
        heads = pl.ds(h * HDIM, HDIM)
        norm = acc[h, :, HDIM:]
        result = (acc[h, :, :HDIM] / norm).astype(BF16)
        o_ref[:, heads] = result
        lse[h] = mb[4, h] * LOG2_SCALE + jnp.log2(norm)
        total = jnp.sum(gh[h].astype(F32) * result.astype(F32), axis=1, keepdims=True)
        corr[h] = jnp.broadcast_to(total, (ROWS, HDIM))

    av[...] = jnp.zeros_like(av)

    def gk_y(j, r):
        return remote(pk.at[4 * j + r], rk.at[j - 1, r - 1], bky, (j - 1, r - 1), along_y(-j))

    def gv_x(i, c):
        return remote(pv.at[c * 5 + 4 - i], rv.at[i - 1, c], bvx, (i - 1, c), along_x(-i))

    def scale_group(slot):
        for h in range(HEADS):
            factor = jnp.exp2(mb[slot, h] * LOG2_SCALE - lse[h])
            scaled = (gh[h].astype(F32) * factor).astype(BF16)
            gs[h] = scaled
            gt[:, pl.ds(h * ROWS, ROWS)] = scaled.T
            acc[h, :, :HDIM] = corr[h] * factor

    def backward(k, v):
        for h in range(HEADS):
            rows = pl.ds(h * ROWS, ROWS)
            dprob = dot(gs[h], vb[v], 1, 1)
            shift = acc[h, :, :HDIM]
            shift = jnp.concatenate([shift, shift], axis=1)
            db[k, rows, :] = (eb[k, rows, :].astype(F32) * (dprob - shift)).astype(BF16)
        value_term = dot(gt[...], eb[k], 1, 0)
        key_term = dot(qt[...], db[k], 1, 0)
        return key_term, value_term

    @pl.loop(1, 5)
    def _(step):
        j = lax.rem(step, 4)
        column = lax.rem(y - j + 4, 4)
        wrap = (j > y).astype(jnp.int32)
        first = jnp.minimum(j, 1)
        scale_group(j + 1)

        @pl.loop(0, 4)
        def _(n):
            r = first + n
            row = r - wrap
            key_term, value_term = backward(4 * j + r, column * 5 + row)

            @pl.when(j > 0)
            def _():
                pk[4 * j + r] = key_term.astype(BF16)
                if COMM:
                    gk_y(j, r).start()

            @pl.when(j == 0)
            def _():
                ak[r] = key_term

            @pl.when((row > 0) & (row < 4))
            def _():
                pv[column * 5 + row] = value_term.astype(BF16)
                if COMM:
                    gv_x(4 - row, column).start()

            @pl.when((row == 0) | (row == 4))
            def _():
                av[row // 4, column] = value_term

    scale_group(0)
    key_term, value_term = backward(4, y * 5 + 4)
    ak[4] = key_term
    av[1, y] = value_term

    def gk_x(i):
        return remote(sk.at[i - 1], rk2.at[i - 1], bkx, (i - 1,), along_x(-i))

    def gv_y(j, old):
        return remote(sv.at[j - 1, old], rv2.at[j - 1, old], bvy, (j - 1, old), along_y(-j))

    def gk_cross():
        return remote(sk3, rk3, bkc, (0,), behind)

    def gv_cross():
        return remote(sv3, rv3, bvc, (0,), behind)

    if COMM:
        for j in (1, 2, 3):
            for r in (1, 2, 3, 4):
                gk_y(j, r).wait_recv()
        for h in (1, 2, 3, 0, 4):
            total = ak[h]
            for j in (1, 2, 3):
                wrap = (y + j >= 4).astype(jnp.int32)
                if h in (1, 2, 3):
                    total = total + rk[j - 1, h + wrap - 1].astype(F32)
                else:
                    hit = (wrap == 1) if h == 0 else (wrap == 0)
                    total = total + jnp.where(hit, rk[j - 1, 0 if h == 0 else 3].astype(F32), 0.0)
            if h in (1, 2, 3):
                sk[4 - h - 1] = total.astype(BF16)
                gk_x(4 - h).start()
            else:
                ak[h] = total
        for i in (1, 2, 3):
            for c in range(4):
                gv_x(i, c).wait_recv()
        for j in (1, 2, 3, 0):
            column = lax.rem(y - j + 4, 4)
            for old in (0, 1):
                total = av[1 - old, column]
                for i in (1, 2, 3):
                    hit = (x + i >= 4) if old else (x + i < 4)
                    total = total + jnp.where(hit, rv[i - 1, column].astype(F32), 0.0)
                if j > 0:
                    sv[j - 1, old] = total.astype(BF16)
                    gv_y(j, old).start()
                else:
                    av[1 - old, column] = total

    for h in range(HEADS):
        total = None
        for k in range(17):
            part = dot(db[k, pl.ds(h * ROWS, ROWS), :], kb[k], 1, 0)
            total = part if total is None else total + part
        dq_ref[:, pl.ds(h * HDIM, HDIM)] = (total * SCALE).astype(BF16)

    key_total, value_total = ak[4], av[1, y]
    if COMM:
        key_old = ak[0]
        for i in (1, 2, 3):
            gk_x(i).wait_recv()
            arrived = rk2[i - 1].astype(F32)
            key_old = key_old + jnp.where(x + i >= 4, arrived, 0.0)
            key_total = key_total + jnp.where(x + i < 4, arrived, 0.0)
        sk3[...] = key_old.astype(BF16)
        gk_cross().start()
        value_old = av[0, y]
        for j in (1, 2, 3):
            gv_y(j, 1).wait_recv()
            value_old = value_old + rv2[j - 1, 1].astype(F32)
        sv3[...] = value_old.astype(BF16)
        gv_cross().start()
        for j in (1, 2, 3):
            gv_y(j, 0).wait_recv()
            value_total = value_total + rv2[j - 1, 0].astype(F32)
        gk_cross().wait_recv()
        key_total = key_total + rk3[...].astype(F32)
        gv_cross().wait_recv()
        value_total = value_total + rv3[...].astype(F32)
    dk_ref[...] = (key_total * SCALE).T.astype(BF16)
    dv_ref[...] = value_total.T.astype(BF16)

    if COMM:
        k_cross().wait_send()
        v_cross().wait_send()
        for i in (1, 2, 3):
            k_x(i).wait_send()
            for c in range(4):
                v_x(i, c).wait_send()
                gv_x(i, c).wait_send()
            gk_x(i).wait_send()
        for j in (1, 2, 3):
            for r in (1, 2, 3, 4):
                k_y(j, r).wait_send()
                gk_y(j, r).wait_send()
            for old in (0, 1):
                v_y(j, old).wait_send()
                gv_y(j, old).wait_send()
        gk_cross().wait_send()
        gv_cross().wait_send()


def shards(queries, keys, values, grad_out, lengths):
    vmem = pl.BlockSpec(memory_space=pltpu.VMEM)
    block = (ROWS, HDIM)
    turned = (HDIM, ROWS)
    dma = pltpu.SemaphoreType.DMA
    return pl.pallas_call(
        kernel,
        out_shape=(
            jax.ShapeDtypeStruct((ROWS, HEADS * HDIM), BF16),
            jax.ShapeDtypeStruct((ROWS, HEADS * HDIM), BF16),
            jax.ShapeDtypeStruct(block, BF16),
            jax.ShapeDtypeStruct(block, BF16),
        ),
        in_specs=[pl.BlockSpec(memory_space=pltpu.SMEM), vmem, vmem, vmem, vmem],
        out_specs=(vmem, vmem, vmem, vmem),
        scratch_shapes=[
            pltpu.VMEM((17,) + block, BF16),
            pltpu.VMEM((20,) + block, BF16),
            pltpu.VMEM((17,) + block, BF16),
            pltpu.VMEM((HEADS, ROWS, 2 * HDIM), BF16),
            pltpu.VMEM((HDIM, HEADS * ROWS), BF16),
            pltpu.VMEM((HEADS,) + block, BF16),
            pltpu.VMEM((HEADS,) + block, BF16),
            pltpu.VMEM((HDIM, HEADS * ROWS), BF16),
            pltpu.VMEM((17, HEADS * ROWS, ROWS), BF16),
            pltpu.VMEM((17, HEADS * ROWS, ROWS), BF16),
            pltpu.VMEM((5, HEADS) + block, F32),
            pltpu.VMEM((HEADS, ROWS, 2 * HDIM), F32),
            pltpu.VMEM((HEADS,) + block, F32),
            pltpu.VMEM((HEADS,) + block, F32),
            pltpu.VMEM((17,) + turned, BF16),
            pltpu.VMEM((20,) + turned, BF16),
            pltpu.VMEM((3, 4) + turned, BF16),
            pltpu.VMEM((3, 4) + turned, BF16),
            pltpu.VMEM((3,) + turned, BF16),
            pltpu.VMEM((3, 2) + turned, BF16),
            pltpu.VMEM(turned, BF16),
            pltpu.VMEM(turned, BF16),
            pltpu.VMEM((5,) + turned, F32),
            pltpu.VMEM((2, 4) + turned, F32),
            pltpu.VMEM((3,) + turned, BF16),
            pltpu.VMEM((3, 2) + turned, BF16),
            pltpu.VMEM(turned, BF16),
            pltpu.VMEM(turned, BF16),
            dma((2,)),
            dma((2, 1)),
            dma((2, 1)),
            dma((2, 3)),
            dma((2, 3, 4)),
            dma((2, 3, 2)),
            dma((2, 3, 4)),
            dma((2, 3, 4)),
            dma((2, 3, 4)),
            dma((2, 3)),
            dma((2, 3, 2)),
            dma((2, 1)),
            dma((2, 1)),
        ],
        compiler_params=pltpu.CompilerParams(
            collective_id=0 if COMM else None, has_side_effects=COMM, vmem_limit_bytes=67043328
        ),
        name="attention",
    )(lengths, queries, keys, values, grad_out)


def solution(mesh):
    spread = P(("dp", "ctx"), None)
    return jax.shard_map(
        shards,
        mesh=mesh,
        in_specs=(spread, spread, spread, spread, P()),
        out_specs=(spread, spread, spread, spread),
        check_vma=False,
    )
```

profile of v0, /device:TPU:1, one launch (start us, length us, event | category | flops | bytes accessed | tf_op | source)
XLA Modules:
  0.0 81.8 jit_solution(15266964792452622862)
XLA Ops:
  0.6 76.8 %attention.1 = (bf16[256,1024]{1,0:T(8,128)(2,1)}, bf16[256,1024]{1,0:T(8,128)(2,1)}, bf16[256,128]{1,0:T(8,128)(2,1)}, bf16[256,128]{1,0:T(8,128)(2,1)}) custom-call(s32[32]{0:T(128)} %len_ref.1, bf16[256,1024]{1,0:T(8,128)(2,1)} %q_ref.1, bf16[256,128]{1,0:T(8,128)(2,1)} %k_ref.1, bf16[256,128]{1,0:T(8,128)(2,1)} %v_ref.1, bf16[256,1024]{1,0:T(8,128)(2,1)} %g_ref.1), custom_call_target="tpu_custom_call" | custom-call | tf_op jit(solution)/shard_map/attention/pallas_call | solution.py:395
  77.5 0.0 copy-start
  77.5 1.9 %copy.13 = bf16[256,1024]{1,0:T(8,128)(2,1)} copy(bf16[256,1024]{1,0:T(8,128)(2,1)} %get-tuple-element.8) | data formatting | bytes 1048576
  79.4 0.0 copy-done
  79.4 0.0 copy-start.2
  79.4 0.8 copy.14
  80.2 0.1 copy-done.2
  80.3 0.0 copy-start.1
  80.3 0.6 copy.15
  80.9 0.2 copy-done.1
  81.1 0.6 copy.16
Async XLA Ops:
  77.5 1.9 %copy-start = (bf16[256,1024]{1,0:T(8,128)(2,1)S(1)}, bf16[256,1024]{1,0:T(8,128)(2,1)}, u32[]{:S(2)}) copy-start(bf16[256,1024]{1,0:T(8,128)(2,1)} %get-tuple-element.9) | copy-start | bytes 1572868
  79.4 0.9 %copy-start.2 = (bf16[256,128]{1,0:T(8,128)(2,1)S(1)}, bf16[256,128]{1,0:T(8,128)(2,1)}, u32[]{:S(2)}) copy-start(bf16[256,128]{1,0:T(8,128)(2,1)} %get-tuple-element.10) | copy-start | bytes 196612
  80.3 0.9 %copy-start.1 = (bf16[256,128]{1,0:T(8,128)(2,1)S(1)}, bf16[256,128]{1,0:T(8,128)(2,1)}, u32[]{:S(2)}) copy-start(bf16[256,128]{1,0:T(8,128)(2,1)} %get-tuple-element.11) | copy-start | bytes 196612
where the time goes:
time: 82 us; the launch traced here: 81.8 us
  Pallas kernels  76.8 us (94%)
  local copies, waits for them, and re-layouts  4.28 us (5%)
    pallas_call x1, Pallas kernels, shards(): pl.pallas_call(kernel, out_shape=(jax.ShapeDtypeStruct((ROWS, HEADS * HDI...  76.8 us
    unnamed x10, local copies, waits for them, and re-layouts  4.28 us

commit v1 on v0

v1 whole, which is shorter than its diff:
```python
import functools
import math

import jax
import jax.numpy as jnp
from jax import lax
from jax.experimental import pallas as pl
from jax.experimental.pallas import tpu as pltpu
from jax.sharding import PartitionSpec as P

HEADS = 8
HDIM = 128
ROWS = 256
NDOCS = 32
SCALE = float(HDIM) ** -0.5
LOG2_SCALE = SCALE * math.log2(math.e)
BIG = 2.0**20
MESH = pl.DeviceIdType.MESH
F32 = jnp.float32
BF16 = jnp.bfloat16
FWD_UNROLL = 8
OUT_UNROLL = 8
VALUES_AT = 11
COMM = True


def dot(a, b, ca, cb):
    return lax.dot_general(a, b, (((ca,), (cb,)), ((), ())), preferred_element_type=F32)


def kernel(
    len_ref, q_ref, k_ref, v_ref, g_ref, o_ref, dq_ref, dk_ref, dv_ref,
    kb, vb, fk, qa, qt, gh, gs, gt, eb, mb, acc, tot,
    pk, pv, rk, rv, rk2, rv2, ak, av, sk, sv,
    loc, kx, ky, vy, vx, bky, bvx, bkx, bvy,
):
    dp, ctx = lax.axis_index("dp"), lax.axis_index("ctx")
    x, y = ctx // 4, lax.rem(ctx, 4)
    block = dp * 16 + ctx

    def along_x(i, plane=0):
        return (lax.rem(dp + plane + 8, 8), lax.rem(x + i + 4, 4) * 4 + y)

    def along_y(j, plane=0):
        return (lax.rem(dp + plane + 8, 8), x * 4 + lax.rem(y + j + 4, 4))

    def remote(src, dst, sems, index, device):
        return pltpu.make_async_remote_copy(
            src_ref=src, dst_ref=dst, send_sem=sems.at[(0,) + index], recv_sem=sems.at[(1,) + index],
            device_id=device, device_id_type=MESH,
        )

    own = [
        pltpu.make_async_copy(k_ref, kb.at[4], loc.at[0]),
        pltpu.make_async_copy(v_ref, vb.at[y * 5 + 4], loc.at[1]),
    ]
    for copy in own:
        copy.start()
    if COMM:
        barrier = pltpu.get_barrier_semaphore()

        def greet(device):
            pl.semaphore_signal(barrier, inc=1, device_id=device, device_id_type=MESH)

        for i in (1, 2, 3):
            greet(along_x(i))
            greet(along_y(i))
            greet(along_x(i, jnp.where(x + i >= 4, 1, -1)))
            greet(along_y(i, 1))
            greet(along_y(i, -1))
        greet(along_y(0, 1))
        greet(along_y(0, -1))
    for copy in own:
        copy.wait()

    def wraps(at, steps):
        return (at + steps >= 4).astype(jnp.int32)

    def k_x(i):
        return remote(k_ref, kb.at[4 - i], kx, (i - 1,), along_x(i, wraps(x, i)))

    def k_y(j, r):
        return remote(kb.at[r - wraps(y, j)], kb.at[4 * j + r], ky, (j - 1, r - 1), along_y(j))

    def v_y(j, old):
        return remote(v_ref, vb.at[y * 5 + (0 if old else 4)], vy, (j, old), along_y(j, old))

    def v_own(i):
        return remote(v_ref, vb.at[y * 5 + 4 - i], vx, (i - 1, y), along_x(i, wraps(x, i)))

    def v_x(i, c):
        return remote(vb.at[c * 5 + 4 - 4 * wraps(x, i)], vb.at[c * 5 + 4 - i], vx, (i - 1, c), along_x(i))

    v_first = [(j, old) for old in (0, 1) for j in (1, 3, 2)] + [(0, 1)]
    if COMM:
        pl.semaphore_wait(barrier, 17)
        for i in (1, 3, 2, 4):
            k_x(i).start()
        for j, old in v_first:
            v_y(j, old).start()
        for j in (1, 3, 2):
            @pl.when(y + j < 4)
            def _():
                k_y(j, 4).start()
        for i in (1, 3, 2):
            v_own(i).start()

    lane = lax.broadcasted_iota(jnp.int32, (1, HDIM), 1)
    starts = jnp.zeros((1, HDIM), jnp.int32)
    stops = jnp.zeros((1, HDIM), jnp.int32)
    total = jnp.int32(0)
    for d in range(NDOCS):
        starts = jnp.where(lane == d, total, starts)
        total = total + len_ref[d]
        stops = jnp.where(lane == d, total, stops)
    place = lax.broadcasted_iota(jnp.int32, (ROWS, HDIM), 0)

    def member(start):
        position = place + start
        return (position >= starts) & (position < stops)

    query_member = jnp.where(member(block * ROWS), 1.0, 0.0).astype(BF16)
    for h in range(HEADS):
        heads = pl.ds(h * HDIM, HDIM)
        qa[h, :, :HDIM] = q_ref[:, heads]
        qa[h, :, HDIM:] = query_member
        gh[h] = g_ref[:, heads]

    @pl.loop(0, 17)
    def _(index):
        group = jnp.maximum(index - 1, 0) // 4
        back = group + 4 * (4 - (index - 4 * group))
        fk[index] = jnp.where(member((block - back) * ROWS), 0.0, -BIG).astype(BF16)

    def head_rows(h):
        return pl.ds(pl.multiple_of(h * ROWS, ROWS), ROWS)

    def halves(tiles):
        return [t[:, half] for t in tiles for half in (slice(0, HDIM), slice(HDIM, 2 * HDIM))]

    def forward(slot, k0, v0, blocks, ready=None):
        def body(h, carry):
            scores = [
                dot(qa[h], jnp.concatenate([kb[k0 + n], fk[k0 + n]], axis=1), 1, 1) for n in range(blocks)
            ]
            if slot is None:
                row = lax.broadcasted_iota(jnp.int32, (ROWS, ROWS), 0)
                column = lax.broadcasted_iota(jnp.int32, (ROWS, ROWS), 1)
                scores = [jnp.where(column <= row, scores[0], -BIG)]
            top = functools.reduce(jnp.maximum, halves(scores))
            top = jnp.max(top, axis=1, keepdims=True)
            if slot is None:
                peak = jnp.broadcast_to(top, (ROWS, HDIM))
                mb[0, h] = peak
            else:
                before = mb[slot - 1, h]
                peak = jnp.maximum(before, top)
                mb[slot, h] = peak
            peak2 = jnp.concatenate([peak, peak], axis=1) * LOG2_SCALE
            weights = [jnp.exp2(score * LOG2_SCALE - peak2) for score in scores]
            part = functools.reduce(jnp.add, halves(weights))
            for n in range(blocks):
                eb[k0 + n, head_rows(h), :] = weights[n].astype(BF16)
            if slot is None:
                tot[h] = part
            else:
                tot[h] = tot[h] * jnp.exp2((before - peak) * LOG2_SCALE) + part
            return carry

        def gather(h, carry):
            weights = jnp.concatenate([eb[k0 + n, head_rows(h), :] for n in range(blocks)], axis=1)
            term = dot(weights, vb[pl.ds(v0, blocks)].reshape(blocks * ROWS, HDIM), 1, 0)
            if slot is None:
                acc[h] = term
            else:
                acc[h] = acc[h] * jnp.exp2((mb[slot - 1, h] - mb[slot, h]) * LOG2_SCALE) + term
            return carry

        lax.fori_loop(0, HEADS, body, 0, unroll=FWD_UNROLL)
        if ready is not None:
            ready()
        lax.fori_loop(0, HEADS, gather, 0, unroll=OUT_UNROLL)

    forward(None, 4, y * 5 + 4, 1)

    if COMM:
        for i in (1, 3, 2, 4):
            k_x(i).wait_recv()
        for j in (1, 3, 2):
            @pl.when(y + j >= 4)
            def _():
                k_y(j, 4).start()
            for r in (3, 2, 1):
                k_y(j, r).start()
        for j, old in v_first:
            v_y(j, old).wait_recv()
        for j in (1, 3, 2):
            for i in (1, 3, 2):
                v_x(i, lax.rem(y - j + 4, 4)).start()
        for i in (1, 3, 2):
            v_own(i).wait_recv()

    forward(1, 0, y * 5, 4)

    for h in range(HEADS):
        qt[:, pl.ds(h * ROWS, ROWS)] = q_ref[:, pl.ds(h * HDIM, HDIM)].T

    @pl.loop(0, 3)
    def _(step):
        j = 1 + lax.rem(2 * step, 3)
        column = lax.rem(y - j + 4, 4)
        wrap = (j > y).astype(jnp.int32)
        if COMM:
            for r in (1, 2, 3, 4):
                k_y(j, r).wait_recv()

        def ready():
            for i in (1, 2, 3):
                v_x(i, column).wait_recv()

        forward(step + 2, 4 * j + 1, column * 5 + 1 - wrap, 4, ready if COMM else None)

    for h in range(HEADS):
        heads = pl.ds(h * HDIM, HDIM)
        norm = jnp.broadcast_to(jnp.sum(tot[h], axis=1, keepdims=True), (ROWS, HDIM))
        result = (acc[h] / norm).astype(BF16)
        o_ref[:, heads] = result
        grad = gh[h].astype(F32)
        fix = jnp.sum(grad * result.astype(F32), axis=1, keepdims=True)
        top = mb[4, h] * LOG2_SCALE + jnp.log2(norm)
        for slot in range(5):
            factor = jnp.exp2(mb[slot, h] * LOG2_SCALE - top)
            mb[slot, h] = factor * fix
            scaled = (grad * factor).astype(BF16)
            gs[slot, h] = scaled
            gt[slot, :, pl.ds(h * ROWS, ROWS)] = scaled.T

    def slot_of(j):
        return jnp.where(j == 0, 1, 2 + lax.rem(2 * (j - 1), 3))

    def gk_y(j, r):
        return remote(pk.at[4 * j + r], rk.at[j - 1, r - 1], bky, (j - 1, r - 1), along_y(-j))

    def gv_x(i, c):
        return remote(pv.at[c * 5 + 4 - i], rv.at[i - 1, c], bvx, (i - 1, c), along_x(-i))

    def gk_x(i):
        back = (x < i).astype(jnp.int32)
        return remote(sk.at[i - 1], rk2.at[i - 1], bkx, (i - 1,), along_x(-i, -back))

    def gv_y(j, old):
        return remote(sv.at[j, old], rv2.at[j, old], bvy, (j, old), along_y(-j, -old))

    @pl.loop(0, 12)
    def _(n):
        column = n // 3
        row = 1 + lax.rem(lax.rem(n, 3) + 1, 3)
        j = lax.rem(y - column + 4, 4)
        wrap = (j > y).astype(jnp.int32)
        term = dot(gt[slot_of(j)], eb[4 * j + row + wrap], 1, 0)
        pv[column * 5 + row] = term.astype(BF16)
        if COMM:
            gv_x(4 - row, column).start()

    av[...] = jnp.zeros_like(av)
    av[1, y] = dot(gt[0], eb[4], 1, 0)

    @pl.loop(0, 4)
    def _(j):
        column = lax.rem(y - j + 4, 4)
        wrap = (j > y).astype(jnp.int32)
        late = jnp.where((j > 0) & (wrap == 0), 1, 0)
        av[late, column] = dot(gt[slot_of(j)], eb[4 * j + 4 * late + wrap], 1, 0)

    def values_second():
        for i in (1, 3, 2):
            for c in range(4):
                gv_x(i, c).wait_recv()
        for j in (2, 1, 3, 0):
            column = lax.rem(y - j + 4, 4)
            for old in (1, 0):
                total = av[1 - old, column]
                for i in (1, 2, 3):
                    hit = (x + i >= 4) if old else (x + i < 4)
                    total = total + jnp.where(hit, rv[i - 1, column].astype(F32), 0.0)
                if j > 0 or old:
                    sv[j, old] = total.astype(BF16)
                    gv_y(j, old).start()
                else:
                    av[1, column] = total

    def backward(k, v, slot):
        for h in range(HEADS):
            rows = pl.ds(h * ROWS, ROWS)
            dprob = dot(gs[slot, h], vb[v], 1, 1)
            shift = mb[slot, h]
            shift = jnp.concatenate([shift, shift], axis=1)
            eb[k, rows, :] = (eb[k, rows, :].astype(F32) * (dprob - shift)).astype(BF16)
        return dot(qt[...], eb[k], 1, 0)

    def pass_keys(n):
        r = 1 + n // 3
        j = 1 + lax.rem(lax.rem(n, 3) + 1, 3)
        column = lax.rem(y - j + 4, 4)
        wrap = (j > y).astype(jnp.int32)
        pk[4 * j + r] = backward(4 * j + r, column * 5 + r - wrap, slot_of(j)).astype(BF16)
        if COMM:
            gk_y(j, r).start()

    @pl.loop(0, 12)
    def _(n):
        pass_keys(n)
        if COMM:
            @pl.when(n == VALUES_AT)
            def _():
                values_second()

    @pl.loop(0, 5)
    def _(r):
        ak[r] = backward(r, y * 5 + r, jnp.where(r == 4, 0, 1))

    if COMM:
        for j in (1, 2, 3):
            for r in (1, 2, 3, 4):
                gk_y(j, r).wait_recv()
        for h in (0, 2, 1, 3, 4):
            total = ak[h]
            for j in (1, 2, 3):
                wrap = (y + j >= 4).astype(jnp.int32)
                if h in (1, 2, 3):
                    total = total + rk[j - 1, h + wrap - 1].astype(F32)
                else:
                    hit = (wrap == 1) if h == 0 else (wrap == 0)
                    total = total + jnp.where(hit, rk[j - 1, 0 if h == 0 else 3].astype(F32), 0.0)
            if h < 4:
                sk[4 - h - 1] = total.astype(BF16)
                gk_x(4 - h).start()
            else:
                ak[h] = total

    def query_grad(h, carry):
        total = None
        for k in range(17):
            part = dot(eb[k, head_rows(h), :], kb[k], 1, 0)
            total = part if total is None else total + part
        dq_ref[:, pl.ds(pl.multiple_of(h * HDIM, HDIM), HDIM)] = (total * SCALE).astype(BF16)
        return carry

    lax.fori_loop(0, 4, query_grad, 0)

    value_total = av[1, y]
    if COMM:
        for j, old in v_first:
            gv_y(j, old).wait_recv()
            value_total = value_total + rv2[j, old].astype(F32)
    dv_ref[...] = value_total.T.astype(BF16)

    lax.fori_loop(4, HEADS, query_grad, 0)

    key_total = ak[4]
    if COMM:
        for i in (1, 2, 3, 4):
            gk_x(i).wait_recv()
            key_total = key_total + rk2[i - 1].astype(F32)
    dk_ref[...] = (key_total * SCALE).T.astype(BF16)

    if COMM:
        for i in (1, 2, 3, 4):
            k_x(i).wait_send()
            gk_x(i).wait_send()
        for i in (1, 2, 3):
            v_own(i).wait_send()
            for j in (1, 2, 3):
                v_x(i, lax.rem(y - j + 4, 4)).wait_send()
            for c in range(4):
                gv_x(i, c).wait_send()
        for j in (1, 2, 3):
            for r in (1, 2, 3, 4):
                k_y(j, r).wait_send()
                gk_y(j, r).wait_send()
        for j, old in v_first:
            v_y(j, old).wait_send()
            gv_y(j, old).wait_send()


CHUNKS = [(n, c) for n in (0, 1) for c in range(4)] + [(2, 0), (3, 0)]


def deliver(*refs):
    given, taken, held, sems = refs[:4], refs[4:8], refs[8:12], refs[12]

    def piece(n, c):
        return pl.ds(c * (ROWS // 4), ROWS // 4) if n < 2 else pl.ds(0, ROWS)

    def fetch(at, n, c):
        return pltpu.make_async_copy(given[n].at[piece(n, c)], held[n].at[piece(n, c)], sems.at[0, at])

    def store(at, n, c):
        return pltpu.make_async_copy(held[n].at[piece(n, c)], taken[n].at[piece(n, c)], sems.at[1, at])

    for at, chunk in enumerate(CHUNKS):
        fetch(at, *chunk).start()
    for at, chunk in enumerate(CHUNKS):
        fetch(at, *chunk).wait()
        store(at, *chunk).start()
    for at, chunk in enumerate(CHUNKS):
        store(at, *chunk).wait()


def shards(queries, keys, values, grad_out, lengths):
    vmem = pl.BlockSpec(memory_space=pltpu.VMEM)
    block = (ROWS, HDIM)
    turned = (HDIM, ROWS)
    dma = pltpu.SemaphoreType.DMA
    shapes = (
        jax.ShapeDtypeStruct((ROWS, HEADS * HDIM), BF16),
        jax.ShapeDtypeStruct((ROWS, HEADS * HDIM), BF16),
        jax.ShapeDtypeStruct(block, BF16),
        jax.ShapeDtypeStruct(block, BF16),
    )
    results = pl.pallas_call(
        kernel,
        out_shape=shapes,
        in_specs=[pl.BlockSpec(memory_space=pltpu.SMEM), vmem, vmem, vmem, vmem],
        out_specs=(vmem, vmem, vmem, vmem),
        scratch_shapes=[
            pltpu.VMEM((17,) + block, BF16),
            pltpu.VMEM((20,) + block, BF16),
            pltpu.VMEM((17,) + block, BF16),
            pltpu.VMEM((HEADS, ROWS, 2 * HDIM), BF16),
            pltpu.VMEM((HDIM, HEADS * ROWS), BF16),
            pltpu.VMEM((HEADS,) + block, BF16),
            pltpu.VMEM((5, HEADS) + block, BF16),
            pltpu.VMEM((5, HDIM, HEADS * ROWS), BF16),
            pltpu.VMEM((17, HEADS * ROWS, ROWS), BF16),
            pltpu.VMEM((5, HEADS) + block, F32),
            pltpu.VMEM((HEADS,) + block, F32),
            pltpu.VMEM((HEADS,) + block, F32),
            pltpu.VMEM((17,) + turned, BF16),
            pltpu.VMEM((20,) + turned, BF16),
            pltpu.VMEM((3, 4) + turned, BF16),
            pltpu.VMEM((3, 4) + turned, BF16),
            pltpu.VMEM((4,) + turned, BF16),
            pltpu.VMEM((4, 2) + turned, BF16),
            pltpu.VMEM((5,) + turned, F32),
            pltpu.VMEM((2, 4) + turned, F32),
            pltpu.VMEM((4,) + turned, BF16),
            pltpu.VMEM((4, 2) + turned, BF16),
            dma((2,)),
            dma((2, 4)),
            dma((2, 3, 4)),
            dma((2, 4, 2)),
            dma((2, 3, 4)),
            dma((2, 3, 4)),
            dma((2, 3, 4)),
            dma((2, 4)),
            dma((2, 4, 2)),
        ],
        compiler_params=pltpu.CompilerParams(
            collective_id=0 if COMM else None, has_side_effects=COMM, vmem_limit_bytes=67043328
        ),
        name="attention",
    )(lengths, queries, keys, values, grad_out)
    away = pl.BlockSpec(memory_space=pl.ANY)
    return pl.pallas_call(
        deliver,
        out_shape=shapes,
        in_specs=[away] * 4,
        out_specs=(away,) * 4,
        scratch_shapes=[pltpu.VMEM(shape.shape, BF16) for shape in shapes] + [dma((2, len(CHUNKS)))],
        name="deliver",
    )(*results)


def solution(mesh):
    spread = P(("dp", "ctx"), None)
    return jax.shard_map(
        shards,
        mesh=mesh,
        in_specs=(spread, spread, spread, spread, P()),
        out_specs=(spread, spread, spread, spread),
        check_vma=False,
    )
```

time: 82 us -> 71.9 us (0.88)
  the two profiles are of different devices: /device:TPU:1 before, /device:TPU:0 now
where the time goes in v1:
time: 71.9 us; the launch traced here: 71.7 us
  Pallas kernels  70.9 us (99%)
  between operations  0.8 us (1%)
    pallas_call x1, Pallas kernels, shards(): pl.pallas_call(kernel, out_shape=shapes, in_specs=[pl.BlockSpec(memory_sp...  68.7 us
    pallas_call x1, Pallas kernels, shards(): pl.pallas_call(deliver, out_shape=shapes, in_specs=[away] * 4, out_specs=...  2.16 us

profile of v1, /device:TPU:0, one launch (start us, length us, event | category | flops | bytes accessed | tf_op | source)
XLA Modules:
  0.0 71.7 jit_solution(14447374464380094147)
XLA Ops:
  0.6 68.7 %attention.1 = (bf16[256,1024]{1,0:T(8,128)(2,1)}, bf16[256,1024]{1,0:T(8,128)(2,1)}, bf16[256,128]{1,0:T(8,128)(2,1)}, bf16[256,128]{1,0:T(8,128)(2,1)}) custom-call(s32[32]{0:T(128)} %len_ref.1, bf16[256,1024]{1,0:T(8,128)(2,1)} %q_ref.1, bf16[256,128]{1,0:T(8,128)(2,1)} %k_ref.1, bf16[256,128]{1,0:T(8,128)(2,1)} %v_ref.1, bf16[256,1024]{1,0:T(8,128)(2,1)} %g_ref.1), custom_call_target="tpu_custom_call" | custom-call | tf_op jit(solution)/shard_map/attention/pallas_call | solution.py:421
  69.4 2.2 %deliver.1 = (bf16[256,1024]{1,0:T(8,128)(2,1)}, bf16[256,1024]{1,0:T(8,128)(2,1)}, bf16[256,128]{1,0:T(8,128)(2,1)}, bf16[256,128]{1,0:T(8,128)(2,1)}) custom-call(bf16[256,1024]{1,0:T(8,128)(2,1)} %get-tuple-element.8.refs_0_, bf16[256,1024]{1,0:T(8,128)(2,1)} %get-tuple-element.9.refs_1_, bf16[256,128]{1,0:T(8,128)(2,1)} %get-tuple-element.10.refs_2_, ...), custom_call_target="tpu_custom_call" | custom-call | tf_op jit(solution)/shard_map/deliver/pallas_call | solution.py:465

commit v2 on v1

--- a/solution.py
+++ b/solution.py
@@ -21,6 +21,7 @@
 FWD_UNROLL = 8
 OUT_UNROLL = 8
 VALUES_AT = 11
+TAIL_AT = 2
 COMM = True
 
 
@@ -30,7 +31,7 @@
 
 def kernel(
     len_ref, q_ref, k_ref, v_ref, g_ref, o_ref, dq_ref, dk_ref, dv_ref,
-    kb, vb, fk, qa, qt, gh, gs, gt, eb, mb, acc, tot,
+    kb, vb, fk, qa, qt, gh, gs, gt, eb, mb, tot,
     pk, pv, rk, rv, rk2, rv2, ak, av, sk, sv,
     loc, kx, ky, vy, vx, bky, bvx, bkx, bvy,
 ):
@@ -51,8 +52,8 @@
         )
 
     own = [
-        pltpu.make_async_copy(k_ref, kb.at[4], loc.at[0]),
-        pltpu.make_async_copy(v_ref, vb.at[y * 5 + 4], loc.at[1]),
+        pltpu.make_async_copy(k_ref, kb.at[y * 5 + 4], loc.at[0]),
+        pltpu.make_async_copy(v_ref, vb.at[4], loc.at[1]),
     ]
     for copy in own:
         copy.start()
@@ -66,8 +67,6 @@
             greet(along_x(i))
             greet(along_y(i))
             greet(along_x(i, jnp.where(x + i >= 4, 1, -1)))
-            greet(along_y(i, 1))
-            greet(along_y(i, -1))
         greet(along_y(0, 1))
         greet(along_y(0, -1))
     for copy in own:
@@ -76,34 +75,30 @@
     def wraps(at, steps):
         return (at + steps >= 4).astype(jnp.int32)
 
-    def k_x(i):
-        return remote(k_ref, kb.at[4 - i], kx, (i - 1,), along_x(i, wraps(x, i)))
-
-    def k_y(j, r):
-        return remote(kb.at[r - wraps(y, j)], kb.at[4 * j + r], ky, (j - 1, r - 1), along_y(j))
-
-    def v_y(j, old):
-        return remote(v_ref, vb.at[y * 5 + (0 if old else 4)], vy, (j, old), along_y(j, old))
-
-    def v_own(i):
-        return remote(v_ref, vb.at[y * 5 + 4 - i], vx, (i - 1, y), along_x(i, wraps(x, i)))
-
-    def v_x(i, c):
-        return remote(vb.at[c * 5 + 4 - 4 * wraps(x, i)], vb.at[c * 5 + 4 - i], vx, (i - 1, c), along_x(i))
-
-    v_first = [(j, old) for old in (0, 1) for j in (1, 3, 2)] + [(0, 1)]
-    if COMM:
-        pl.semaphore_wait(barrier, 17)
+    def v_x(i):
+        return remote(v_ref, vb.at[4 - i], vx, (i - 1,), along_x(i, wraps(x, i)))
+
+    def v_y(j, r):
+        return remote(vb.at[r - wraps(y, j)], vb.at[4 * j + r], vy, (j - 1, r - 1), along_y(j))
+
+    def k_y(j):
+        return remote(k_ref, kb.at[y * 5 + 4], ky, (j - 1,), along_y(j))
+
+    def k_x(i, c):
+        return remote(kb.at[c * 5 + 4], kb.at[c * 5 + 4 - i], kx, (i - 1, c), along_x(i, wraps(x, i)))
+
+    if COMM:
+        pl.semaphore_wait(barrier, 11)
+        for j in (1, 3, 2):
+            k_y(j).start()
         for i in (1, 3, 2, 4):
-            k_x(i).start()
-        for j, old in v_first:
-            v_y(j, old).start()
+            k_x(i, y).start()
+        for i in (1, 3, 2, 4):
+            v_x(i).start()
         for j in (1, 3, 2):
             @pl.when(y + j < 4)
             def _():
-                k_y(j, 4).start()
-        for i in (1, 3, 2):
-            v_own(i).start()
+                v_y(j, 4).start()
 
     lane = lax.broadcasted_iota(jnp.int32, (1, HDIM), 1)
     starts = jnp.zeros((1, HDIM), jnp.int32)
@@ -138,10 +133,10 @@
     def halves(tiles):
         return [t[:, half] for t in tiles for half in (slice(0, HDIM), slice(HDIM, 2 * HDIM))]
 
-    def forward(slot, k0, v0, blocks, ready=None):
+    def forward(slot, k0, c0, blocks):
         def body(h, carry):
             scores = [
-                dot(qa[h], jnp.concatenate([kb[k0 + n], fk[k0 + n]], axis=1), 1, 1) for n in range(blocks)
+                dot(qa[h], jnp.concatenate([kb[c0 + n], fk[k0 + n]], axis=1), 1, 1) for n in range(blocks)
             ]
             if slot is None:
                 row = lax.broadcasted_iota(jnp.int32, (ROWS, ROWS), 0)
@@ -167,38 +162,31 @@
                 tot[h] = tot[h] * jnp.exp2((before - peak) * LOG2_SCALE) + part
             return carry
 
-        def gather(h, carry):
-            weights = jnp.concatenate([eb[k0 + n, head_rows(h), :] for n in range(blocks)], axis=1)
-            term = dot(weights, vb[pl.ds(v0, blocks)].reshape(blocks * ROWS, HDIM), 1, 0)
-            if slot is None:
-                acc[h] = term
-            else:
-                acc[h] = acc[h] * jnp.exp2((mb[slot - 1, h] - mb[slot, h]) * LOG2_SCALE) + term
-            return carry
-
         lax.fori_loop(0, HEADS, body, 0, unroll=FWD_UNROLL)
-        if ready is not None:
-            ready()
-        lax.fori_loop(0, HEADS, gather, 0, unroll=OUT_UNROLL)
 
     forward(None, 4, y * 5 + 4, 1)
 
     if COMM:
+        for j in (1, 3, 2):
+            k_y(j).wait_recv()
+        for j in (1, 3, 2):
+            column = lax.rem(y - j + 4, 4)
+            for i in (1, 3, 2):
+                k_x(i, column).start()
+
+            @pl.when(j > y)
+            def _():
+                k_x(4, column).start()
         for i in (1, 3, 2, 4):
-            k_x(i).wait_recv()
+            v_x(i).wait_recv()
         for j in (1, 3, 2):
             @pl.when(y + j >= 4)
             def _():
-                k_y(j, 4).start()
+                v_y(j, 4).start()
             for r in (3, 2, 1):
-                k_y(j, r).start()
-        for j, old in v_first:
-            v_y(j, old).wait_recv()
-        for j in (1, 3, 2):
-            for i in (1, 3, 2):
-                v_x(i, lax.rem(y - j + 4, 4)).start()
-        for i in (1, 3, 2):
-            v_own(i).wait_recv()
+                v_y(j, r).start()
+        for i in (1, 3, 2, 4):
+            k_x(i, y).wait_recv()
 
     forward(1, 0, y * 5, 4)
 
@@ -209,28 +197,22 @@
     def _(step):
         j = 1 + lax.rem(2 * step, 3)
         column = lax.rem(y - j + 4, 4)
-        wrap = (j > y).astype(jnp.int32)
         if COMM:
-            for r in (1, 2, 3, 4):
-                k_y(j, r).wait_recv()
-
-        def ready():
             for i in (1, 2, 3):
-                v_x(i, column).wait_recv()
-
-        forward(step + 2, 4 * j + 1, column * 5 + 1 - wrap, 4, ready if COMM else None)
+                k_x(i, column).wait_recv()
+
+            @pl.when(j > y)
+            def _():
+                k_x(4, column).wait_recv()
+        forward(step + 2, 4 * j + 1, column * 5 + jnp.where(j > y, 0, 1), 4)
 
     for h in range(HEADS):
-        heads = pl.ds(h * HDIM, HDIM)
         norm = jnp.broadcast_to(jnp.sum(tot[h], axis=1, keepdims=True), (ROWS, HDIM))
-        result = (acc[h] / norm).astype(BF16)
-        o_ref[:, heads] = result
+        top = mb[4, h] * LOG2_SCALE + jnp.log2(norm)
         grad = gh[h].astype(F32)
-        fix = jnp.sum(grad * result.astype(F32), axis=1, keepdims=True)
-        top = mb[4, h] * LOG2_SCALE + jnp.log2(norm)
         for slot in range(5):
             factor = jnp.exp2(mb[slot, h] * LOG2_SCALE - top)
-            mb[slot, h] = factor * fix
+            mb[slot, h] = factor
             scaled = (grad * factor).astype(BF16)
             gs[slot, h] = scaled
             gt[slot, :, pl.ds(h * ROWS, ROWS)] = scaled.T
@@ -242,14 +224,15 @@
         return remote(pk.at[4 * j + r], rk.at[j - 1, r - 1], bky, (j - 1, r - 1), along_y(-j))
 
     def gv_x(i, c):
-        return remote(pv.at[c * 5 + 4 - i], rv.at[i - 1, c], bvx, (i - 1, c), along_x(-i))
+        back = (x < i).astype(jnp.int32)
+        return remote(pv.at[c * 5 + 4 - i], rv.at[i - 1, c], bvx, (i - 1, c), along_x(-i, -back))
 
     def gk_x(i):
         back = (x < i).astype(jnp.int32)
         return remote(sk.at[i - 1], rk2.at[i - 1], bkx, (i - 1,), along_x(-i, -back))
 
-    def gv_y(j, old):
-        return remote(sv.at[j, old], rv2.at[j, old], bvy, (j, old), along_y(-j, -old))
+    def gv_y(j):
+        return remote(sv.at[j - 1], rv2.at[j - 1], bvy, (j - 1,), along_y(-j))
 
     @pl.loop(0, 12)
     def _(n):
@@ -263,36 +246,72 @@
             gv_x(4 - row, column).start()
 
     av[...] = jnp.zeros_like(av)
-    av[1, y] = dot(gt[0], eb[4], 1, 0)
+    av[y] = dot(gt[0], eb[4], 1, 0)
 
     @pl.loop(0, 4)
     def _(j):
         column = lax.rem(y - j + 4, 4)
         wrap = (j > y).astype(jnp.int32)
-        late = jnp.where((j > 0) & (wrap == 0), 1, 0)
-        av[late, column] = dot(gt[slot_of(j)], eb[4 * j + 4 * late + wrap], 1, 0)
+        late = (j > 0) & (j <= y)
+        term = dot(gt[slot_of(j)], eb[4 * j + jnp.where(late, 4, wrap)], 1, 0)
+
+        @pl.when(late)
+        def _():
+            av[column] = term
+
+        @pl.when(jnp.logical_not(late))
+        def _():
+            pv[column * 5] = term.astype(BF16)
+            if COMM:
+                gv_x(4, column).start()
+
+    if COMM:
+        for j in (1, 3, 2):
+            for r in (4, 3, 2, 1):
+                v_y(j, r).wait_recv()
+
+    def output(h, carry):
+        rows = head_rows(h)
+        heads = pl.ds(pl.multiple_of(h * HDIM, HDIM), HDIM)
+        total = mb[0, h] * dot(eb[4, rows, :], vb[4], 1, 0)
+        for j in range(4):
+            slot = 1 if j == 0 else 2 + (2 * (j - 1)) % 3
+            k0 = 4 * j + min(j, 1)
+            weights = jnp.concatenate([eb[k0 + n, rows, :] for n in range(4)], axis=1)
+            total = total + mb[slot, h] * dot(weights, vb[k0 : k0 + 4].reshape(4 * ROWS, HDIM), 1, 0)
+        result = total.astype(BF16)
+        o_ref[:, heads] = result
+        fix = jnp.sum(gh[h].astype(F32) * result.astype(F32), axis=1, keepdims=True)
+        for slot in range(5):
+            mb[slot, h] = mb[slot, h] * fix
+        return carry
+
+    lax.fori_loop(0, HEADS, output, 0, unroll=OUT_UNROLL)
 
     def values_second():
         for i in (1, 3, 2):
             for c in range(4):
                 gv_x(i, c).wait_recv()
+        for c in range(4):
+            @pl.when(c >= y)
+            def _():
+                gv_x(4, c).wait_recv()
         for j in (2, 1, 3, 0):
             column = lax.rem(y - j + 4, 4)
-            for old in (1, 0):
-                total = av[1 - old, column]
-                for i in (1, 2, 3):
-                    hit = (x + i >= 4) if old else (x + i < 4)
-                    total = total + jnp.where(hit, rv[i - 1, column].astype(F32), 0.0)
-                if j > 0 or old:
-                    sv[j, old] = total.astype(BF16)
-                    gv_y(j, old).start()
-                else:
-                    av[1, column] = total
-
-    def backward(k, v, slot):
+            total = av[column]
+            for i in (1, 2, 3):
+                total = total + rv[i - 1, column].astype(F32)
+            total = total + jnp.where(column >= y, rv[3, column].astype(F32), 0.0)
+            if j > 0:
+                sv[j - 1] = total.astype(BF16)
+                gv_y(j).start()
+            else:
+                av[column] = total
+
+    def backward(k, slot):
         for h in range(HEADS):
             rows = pl.ds(h * ROWS, ROWS)
-            dprob = dot(gs[slot, h], vb[v], 1, 1)
+            dprob = dot(gs[slot, h], vb[k], 1, 1)
             shift = mb[slot, h]
             shift = jnp.concatenate([shift, shift], axis=1)
             eb[k, rows, :] = (eb[k, rows, :].astype(F32) * (dprob - shift)).astype(BF16)
@@ -301,9 +320,7 @@
     def pass_keys(n):
         r = 1 + n // 3
         j = 1 + lax.rem(lax.rem(n, 3) + 1, 3)
-        column = lax.rem(y - j + 4, 4)
-        wrap = (j > y).astype(jnp.int32)
-        pk[4 * j + r] = backward(4 * j + r, column * 5 + r - wrap, slot_of(j)).astype(BF16)
+        pk[4 * j + r] = backward(4 * j + r, slot_of(j)).astype(BF16)
         if COMM:
             gk_y(j, r).start()
 
@@ -317,7 +334,19 @@
 
     @pl.loop(0, 5)
     def _(r):
-        ak[r] = backward(r, y * 5 + r, jnp.where(r == 4, 0, 1))
+        ak[r] = backward(r, jnp.where(r == 4, 0, 1))
+
+    def query_grad(h, carry):
+        total = None
+        for k in range(17):
+            j = max(k - 1, 0) // 4
+            at = lax.rem(y - j + 4, 4) * 5 + k - 4 * j - jnp.where(j > y, 1, 0)
+            part = dot(eb[k, head_rows(h), :], kb[at], 1, 0)
+            total = part if total is None else total + part
+        dq_ref[:, pl.ds(pl.multiple_of(h * HDIM, HDIM), HDIM)] = (total * SCALE).astype(BF16)
+        return carry
+
+    lax.fori_loop(0, TAIL_AT, query_grad, 0)
 
     if COMM:
         for j in (1, 2, 3):
@@ -338,49 +367,38 @@
             else:
                 ak[h] = total
 
-    def query_grad(h, carry):
-        total = None
-        for k in range(17):
-            part = dot(eb[k, head_rows(h), :], kb[k], 1, 0)
-            total = part if total is None else total + part
-        dq_ref[:, pl.ds(pl.multiple_of(h * HDIM, HDIM), HDIM)] = (total * SCALE).astype(BF16)
-        return carry
-
-    lax.fori_loop(0, 4, query_grad, 0)
-
-    value_total = av[1, y]
-    if COMM:
-        for j, old in v_first:
-            gv_y(j, old).wait_recv()
-            value_total = value_total + rv2[j, old].astype(F32)
-    dv_ref[...] = value_total.T.astype(BF16)
-
-    lax.fori_loop(4, HEADS, query_grad, 0)
-
-    key_total = ak[4]
-    if COMM:
+    lax.fori_loop(TAIL_AT, HEADS, query_grad, 0)
+
+    value_total, key_total = av[y], ak[4]
+    if COMM:
+        for j in (1, 2, 3):
+            gv_y(j).wait_recv()
+            value_total = value_total + rv2[j - 1].astype(F32)
         for i in (1, 2, 3, 4):
             gk_x(i).wait_recv()
             key_total = key_total + rk2[i - 1].astype(F32)
+    dv_ref[...] = value_total.T.astype(BF16)
     dk_ref[...] = (key_total * SCALE).T.astype(BF16)
 
     if COMM:
         for i in (1, 2, 3, 4):
-            k_x(i).wait_send()
+            v_x(i).wait_send()
             gk_x(i).wait_send()
         for i in (1, 2, 3):
-            v_own(i).wait_send()
-            for j in (1, 2, 3):
-                v_x(i, lax.rem(y - j + 4, 4)).wait_send()
             for c in range(4):
+                k_x(i, c).wait_send()
                 gv_x(i, c).wait_send()
+        for c in range(4):
+            @pl.when(c >= y)
+            def _():
+                k_x(4, c).wait_send()
+                gv_x(4, c).wait_send()
         for j in (1, 2, 3):
             for r in (1, 2, 3, 4):
-                k_y(j, r).wait_send()
+                v_y(j, r).wait_send()
                 gk_y(j, r).wait_send()
-        for j, old in v_first:
-            v_y(j, old).wait_send()
-            gv_y(j, old).wait_send()
+            k_y(j).wait_send()
+            gv_y(j).wait_send()
 
 
 CHUNKS = [(n, c) for n in (0, 1) for c in range(4)] + [(2, 0), (3, 0)]
@@ -424,8 +442,8 @@
         in_specs=[pl.BlockSpec(memory_space=pltpu.SMEM), vmem, vmem, vmem, vmem],
         out_specs=(vmem, vmem, vmem, vmem),
         scratch_shapes=[
+            pltpu.VMEM((20,) + block, BF16),
             pltpu.VMEM((17,) + block, BF16),
-            pltpu.VMEM((20,) + block, BF16),
             pltpu.VMEM((17,) + block, BF16),
             pltpu.VMEM((HEADS, ROWS, 2 * HDIM), BF16),
             pltpu.VMEM((HDIM, HEADS * ROWS), BF16),
@@ -435,26 +453,25 @@
             pltpu.VMEM((17, HEADS * ROWS, ROWS), BF16),
             pltpu.VMEM((5, HEADS) + block, F32),
             pltpu.VMEM((HEADS,) + block, F32),
-            pltpu.VMEM((HEADS,) + block, F32),
             pltpu.VMEM((17,) + turned, BF16),
             pltpu.VMEM((20,) + turned, BF16),
             pltpu.VMEM((3, 4) + turned, BF16),
-            pltpu.VMEM((3, 4) + turned, BF16),
+            pltpu.VMEM((4, 4) + turned, BF16),
             pltpu.VMEM((4,) + turned, BF16),
-            pltpu.VMEM((4, 2) + turned, BF16),
+            pltpu.VMEM((3,) + turned, BF16),
             pltpu.VMEM((5,) + turned, F32),
-            pltpu.VMEM((2, 4) + turned, F32),
+            pltpu.VMEM((4,) + turned, F32),
             pltpu.VMEM((4,) + turned, BF16),
-            pltpu.VMEM((4, 2) + turned, BF16),
+            pltpu.VMEM((3,) + turned, BF16),
             dma((2,)),
+            dma((2, 4, 4)),
+            dma((2, 3)),
+            dma((2, 3, 4)),
             dma((2, 4)),
             dma((2, 3, 4)),
-            dma((2, 4, 2)),
-            dma((2, 3, 4)),
-            dma((2, 3, 4)),
-            dma((2, 3, 4)),
+            dma((2, 4, 4)),
             dma((2, 4)),
-            dma((2, 4, 2)),
+            dma((2, 3)),
         ],
         compiler_params=pltpu.CompilerParams(
             collective_id=0 if COMM else None, has_side_effects=COMM, vmem_limit_bytes=67043328

time: 71.9 us -> 67.8 us (0.943)
  Pallas kernels: 70.9 us -> 66.5 us
    pallas_call x1, Pallas kernels: 68.7 us -> 64.3 us  [shards(): pl.pallas_call(kernel, out_shape=shapes, in_specs=[pl.BlockSpec(memory_sp...]
where the time goes in v2:
time: 67.8 us; the launch traced here: 67.3 us
  Pallas kernels  66.5 us (98%)
  between operations  0.8 us (1%)
    pallas_call x1, Pallas kernels, shards(): pl.pallas_call(kernel, out_shape=shapes, in_specs=[pl.BlockSpec(memory_sp...  64.3 us
    pallas_call x1, Pallas kernels, shards(): pl.pallas_call(deliver, out_shape=shapes, in_specs=[away] * 4, out_specs=...  2.16 us

profile of v2, /device:TPU:0, one launch (start us, length us, event | category | flops | bytes accessed | tf_op | source)
XLA Modules:
  0.0 67.3 jit_solution(6901407468817471185)
XLA Ops:
  0.6 64.3 %attention.1 = (bf16[256,1024]{1,0:T(8,128)(2,1)}, bf16[256,1024]{1,0:T(8,128)(2,1)}, bf16[256,128]{1,0:T(8,128)(2,1)}, bf16[256,128]{1,0:T(8,128)(2,1)}) custom-call(s32[32]{0:T(128)} %len_ref.1, bf16[256,1024]{1,0:T(8,128)(2,1)} %q_ref.1, bf16[256,128]{1,0:T(8,128)(2,1)} %k_ref.1, bf16[256,128]{1,0:T(8,128)(2,1)} %v_ref.1, bf16[256,1024]{1,0:T(8,128)(2,1)} %g_ref.1), custom_call_target="tpu_custom_call" | custom-call | tf_op jit(solution)/shard_map/attention/pallas_call | solution.py:439
  65.0 2.2 %deliver.1 = (bf16[256,1024]{1,0:T(8,128)(2,1)}, bf16[256,1024]{1,0:T(8,128)(2,1)}, bf16[256,128]{1,0:T(8,128)(2,1)}, bf16[256,128]{1,0:T(8,128)(2,1)}) custom-call(bf16[256,1024]{1,0:T(8,128)(2,1)} %get-tuple-element.8.refs_0_, bf16[256,1024]{1,0:T(8,128)(2,1)} %get-tuple-element.9.refs_1_, bf16[256,128]{1,0:T(8,128)(2,1)} %get-tuple-element.10.refs_2_, ...), custom_call_target="tpu_custom_call" | custom-call | tf_op jit(solution)/shard_map/deliver/pallas_call | solution.py:482

commit v3 on v2

--- a/solution.py
+++ b/solution.py
@@ -30,8 +30,8 @@
 
 
 def kernel(
-    len_ref, q_ref, k_ref, v_ref, g_ref, o_ref, dq_ref, dk_ref, dv_ref,
-    kb, vb, fk, qa, qt, gh, gs, gt, eb, mb, tot,
+    len_ref, q_far, k_ref, v_ref, g_far, o_ref, dq_ref, dk_ref, dv_ref,
+    q_ref, g_ref, kb, vb, fk, qa, qt, gh, gs, gt, eb, mb, tot,
     pk, pv, rk, rv, rk2, rv2, ak, av, sk, sv,
     loc, kx, ky, vy, vx, bky, bvx, bkx, bvy,
 ):
@@ -55,7 +55,11 @@
         pltpu.make_async_copy(k_ref, kb.at[y * 5 + 4], loc.at[0]),
         pltpu.make_async_copy(v_ref, vb.at[4], loc.at[1]),
     ]
-    for copy in own:
+    wide = [
+        pltpu.make_async_copy(q_far, q_ref, loc.at[2]),
+        pltpu.make_async_copy(g_far, g_ref, loc.at[3]),
+    ]
+    for copy in own + wide:
         copy.start()
     if COMM:
         barrier = pltpu.get_barrier_semaphore()
@@ -114,6 +118,8 @@
         position = place + start
         return (position >= starts) & (position < stops)
 
+    for copy in wide:
+        copy.wait()
     query_member = jnp.where(member(block * ROWS), 1.0, 0.0).astype(BF16)
     for h in range(HEADS):
         heads = pl.ds(h * HDIM, HDIM)
@@ -164,12 +170,9 @@
 
         lax.fori_loop(0, HEADS, body, 0, unroll=FWD_UNROLL)
 
-    forward(None, 4, y * 5 + 4, 1)
-
     if COMM:
         for j in (1, 3, 2):
             k_y(j).wait_recv()
-        for j in (1, 3, 2):
             column = lax.rem(y - j + 4, 4)
             for i in (1, 3, 2):
                 k_x(i, column).start()
@@ -177,6 +180,10 @@
             @pl.when(j > y)
             def _():
                 k_x(4, column).start()
+
+    forward(None, 4, y * 5 + 4, 1)
+
+    if COMM:
         for i in (1, 3, 2, 4):
             v_x(i).wait_recv()
         for j in (1, 3, 2):
@@ -427,6 +434,7 @@
 
 def shards(queries, keys, values, grad_out, lengths):
     vmem = pl.BlockSpec(memory_space=pltpu.VMEM)
+    away = pl.BlockSpec(memory_space=pl.ANY)
     block = (ROWS, HDIM)
     turned = (HDIM, ROWS)
     dma = pltpu.SemaphoreType.DMA
@@ -439,9 +447,11 @@
     results = pl.pallas_call(
         kernel,
         out_shape=shapes,
-        in_specs=[pl.BlockSpec(memory_space=pltpu.SMEM), vmem, vmem, vmem, vmem],
+        in_specs=[pl.BlockSpec(memory_space=pltpu.SMEM), away, vmem, vmem, away],
         out_specs=(vmem, vmem, vmem, vmem),
         scratch_shapes=[
+            pltpu.VMEM((ROWS, HEADS * HDIM), BF16),
+            pltpu.VMEM((ROWS, HEADS * HDIM), BF16),
             pltpu.VMEM((20,) + block, BF16),
             pltpu.VMEM((17,) + block, BF16),
             pltpu.VMEM((17,) + block, BF16),
@@ -463,7 +473,7 @@
             pltpu.VMEM((4,) + turned, F32),
             pltpu.VMEM((4,) + turned, BF16),
             pltpu.VMEM((3,) + turned, BF16),
-            dma((2,)),
+            dma((4,)),
             dma((2, 4, 4)),
             dma((2, 3)),
             dma((2, 3, 4)),
@@ -478,7 +488,6 @@
         ),
         name="attention",
     )(lengths, queries, keys, values, grad_out)
-    away = pl.BlockSpec(memory_space=pl.ANY)
     return pl.pallas_call(
         deliver,
         out_shape=shapes,

time: 67.8 us -> 66.7 us (0.984)
  Pallas kernels: 66.5 us -> 65.8 us
    pallas_call x1, Pallas kernels: 64.3 us -> 63.6 us  [shards(): pl.pallas_call(kernel, out_shape=shapes, in_specs=[pl.BlockSpec(memory_sp...]
where the time goes in v3:
time: 66.7 us; the launch traced here: 66.6 us
  Pallas kernels  65.8 us (99%)
  between operations  0.8 us (1%)
    pallas_call x1, Pallas kernels, shards(): pl.pallas_call(kernel, out_shape=shapes, in_specs=[pl.BlockSpec(memory_sp...  63.6 us
    pallas_call x1, Pallas kernels, shards(): pl.pallas_call(deliver, out_shape=shapes, in_specs=[away] * 4, out_specs=...  2.16 us

profile of v3, /device:TPU:0, one launch (start us, length us, event | category | flops | bytes accessed | tf_op | source)
XLA Modules:
  0.0 66.6 jit_solution(4979462098208935858)
XLA Ops:
  0.6 63.6 %attention.1 = (bf16[256,1024]{1,0:T(8,128)(2,1)}, bf16[256,1024]{1,0:T(8,128)(2,1)}, bf16[256,128]{1,0:T(8,128)(2,1)}, bf16[256,128]{1,0:T(8,128)(2,1)}) custom-call(s32[32]{0:T(128)} %len_ref.1, bf16[256,1024]{1,0:T(8,128)(2,1)} %q_far.1, bf16[256,128]{1,0:T(8,128)(2,1)} %k_ref.1, bf16[256,128]{1,0:T(8,128)(2,1)} %v_ref.1, bf16[256,1024]{1,0:T(8,128)(2,1)} %g_far.1), custom_call_target="tpu_custom_call" | custom-call | tf_op jit(solution)/shard_map/attention/pallas_call | solution.py:447
  64.2 2.2 %deliver.1 = (bf16[256,1024]{1,0:T(8,128)(2,1)}, bf16[256,1024]{1,0:T(8,128)(2,1)}, bf16[256,128]{1,0:T(8,128)(2,1)}, bf16[256,128]{1,0:T(8,128)(2,1)}) custom-call(bf16[256,1024]{1,0:T(8,128)(2,1)} %get-tuple-element.8.refs_0_, bf16[256,1024]{1,0:T(8,128)(2,1)} %get-tuple-element.9.refs_1_, bf16[256,128]{1,0:T(8,128)(2,1)} %get-tuple-element.10.refs_2_, ...), custom_call_target="tpu_custom_call" | custom-call | tf_op jit(solution)/shard_map/deliver/pallas_call | solution.py:491
